TPU v7x, 32 devices: a whole 2x2x4 slice. The times are simulated.
32 devices in a mesh: col: 16 (over z, x, core), tok: 2 (over y).
Axes of the slice: x: 2, y: 2, z: 4, core: 2. Of those that a mesh axis runs over, the one named last changes fastest.
Arguments:
- acts: bfloat16 [512, 8192], P('tok', 'col'), may hold values from -6 to 6
- grad_out: bfloat16 [512, 8192], P('tok', 'col'), may hold values from -0.19921875 to 0.19921875
- left_factor: float32 [8, 8192, 1024], P('tok', 'col'), may hold values from -6 to 6
- right_factor: float32 [8, 8192, 1024], P('tok', 'col'), may hold values from -6 to 6
- left_basis: bfloat16 [8, 8192, 1024], P('tok', 'col'), may hold values from -0.1875 to 0.1875
- right_basis: bfloat16 [8, 8192, 1024], P('tok', 'col'), may hold values from -0.1875 to 0.1875
- moment: float32 [8192, 8192], P('tok', 'col'), may hold values from -2 to 2
- second: float32 [8192, 8192], P('tok', 'col'), may hold values from 0.05 to 2
Outputs:
- left_out: float32 [8, 8192, 1024], P('tok', 'col')
- right_out: float32 [8, 8192, 1024], P('tok', 'col')
- moment_out: float32 [8192, 8192], P('tok', 'col')
- second_out: float32 [8192, 8192], P('tok', 'col')
- update: bfloat16 [8192, 8192], P('tok', 'col')
All inputs are finite; a program needn't handle non-finite values.
Results may differ from a plain program's by a relative error of at most 0.0075.
Values may be sent and summed in bfloat16 or wider, within the bound.
No kernel may reach another device: no remote copies, remote signals or barrier semaphores. Data moves between devices by JAX's collectives and lax.ppermute only.
A program may use at most 192 MiB of HBM per device.

v0:
```python
import jax
import jax.numpy as jnp
from jax import lax
from jax.sharding import PartitionSpec as P

B = 1024
shampoo_beta = 0.95
first_beta = 0.9
second_beta = 0.95
first_corr = 1.0 - 0.9**4
second_corr = 1.0 - 0.95**4
epsilon = 1e-08


def swapped(array, axis, distance):
    return lax.ppermute(array, axis, [(i, i ^ 1 << distance) for i in range(lax.axis_size(axis))])


def join_pair(current, incoming, axis, lower):
    width = current.shape[axis]
    shape = list(current.shape)
    shape[axis] = 2 * width
    joined = jnp.zeros(shape, current.dtype)
    mine_at = jnp.where(lower, 0, width)
    theirs_at = width - mine_at
    joined = lax.dynamic_update_slice_in_dim(joined, current, mine_at, axis)
    return lax.dynamic_update_slice_in_dim(joined, incoming, theirs_at, axis)


def shards(acts, grad_out, left_factor, right_factor, left_basis, right_basis, moment, second):
    width = grad_out.shape[1]
    blocks = left_factor.shape[0]
    groups = B // width
    nbits = groups.bit_length() - 1
    member = lax.axis_index("col") % groups
    contract = (((0,), (0,)), ((), ()))
    whole = lax.all_gather(acts, "col", axis=1, tiled=True)
    block_rows = lax.all_to_all(whole, "tok", split_axis=1, concat_axis=0, tiled=True)
    all_grads = lax.all_gather(grad_out, "tok", axis=0, tiled=True)
    grad = lax.dot_general(block_rows, all_grads, contract, preferred_element_type=jnp.float32)
    own = grad.astype(jnp.bfloat16).reshape(blocks, B, width)
    tiles, left_full, right_full = (own, left_basis, right_basis)
    for bit in range(nbits):
        other = swapped((tiles, left_full, right_full), "col", bit)
        lower = member >> bit & 1 == 0
        tiles = join_pair(tiles, other[0], 2, lower)
        left_full = join_pair(left_full, other[1], 1, lower)
        right_full = join_pair(right_full, other[2], 1, lower)
    right_cols = lax.dynamic_slice_in_dim(right_full, member * width, width, 2)
    mixed = jnp.einsum(
        "nab,nbc->nac", tiles, right_cols, preferred_element_type=jnp.float32
    ).astype(jnp.bfloat16)
    lead = lax.dynamic_slice_in_dim(tiles, member * width, width, 1)
    left_new = shampoo_beta * left_factor + (1.0 - shampoo_beta) * jnp.einsum(
        "nab,ncb->nac", lead, tiles, preferred_element_type=jnp.float32
    )
    right_new = shampoo_beta * right_factor + (1.0 - shampoo_beta) * jnp.einsum(
        "nat,nab->ntb", own, tiles, preferred_element_type=jnp.float32
    )
    rotated = jnp.einsum("nab,nac->nbc", left_full, mixed, preferred_element_type=jnp.float32)
    first_new = first_beta * moment.reshape(blocks, B, width) + (1.0 - first_beta) * rotated
    second_new = (
        second_beta * second.reshape(blocks, B, width) + (1.0 - second_beta) * rotated * rotated
    )
    normed = (first_new / first_corr / (jnp.sqrt(second_new / second_corr) + epsilon)).astype(
        jnp.bfloat16
    )
    steps_full = normed
    for bit in range(nbits):
        other_steps = swapped(steps_full, "col", bit)
        lower = member >> bit & 1 == 0
        steps_full = join_pair(steps_full, other_steps, 2, lower)
    back = jnp.einsum(
        "nab,ncb->nac", steps_full, right_basis, preferred_element_type=jnp.float32
    ).astype(jnp.bfloat16)
    update = jnp.einsum("nab,nbc->nac", left_full, back, preferred_element_type=jnp.float32).astype(
        jnp.bfloat16
    )
    rows = blocks * B
    return (
        left_new,
        right_new,
        first_new.reshape(rows, width),
        second_new.reshape(rows, width),
        update.reshape(rows, width),
    )


def solution(mesh):
    in_specs = (
        P("tok", "col"),
        P("tok", "col"),
        P("tok", "col", None),
        P("tok", "col", None),
        P("tok", "col", None),
        P("tok", "col", None),
        P("tok", "col"),
        P("tok", "col"),
    )
    out_specs = (
        P("tok", "col", None),
        P("tok", "col", None),
        P("tok", "col"),
        P("tok", "col"),
        P("tok", "col"),
    )
    return jax.shard_map(shards, mesh=mesh, in_specs=in_specs, out_specs=out_specs, check_vma=False)
```

profile of v0, /device:TPU:0, one launch (start us, length us, event | category | flops | bytes accessed | tf_op | source)
XLA Modules:
  0.0 273.9 jit_solution(15779307181880031778)
XLA Ops:
  7.2 0.0 copy-start.2
  7.2 0.0 all-gather.2.cloned.1.call-start
  7.2 1.8 copy.17
  9.0 0.0 all-gather.2.cloned.1.call-update
  9.1 54.8 %all-gather.2.cloned.1.call-done = bf16[256,8192]{0,1:T(8,128)(2,1)} async-done(((bf16[256,512]{0,1:T(8,128)(2,1)}), bf16[256,8192]{0,1:T(8,128)(2,1)}) %all-gather.2.cloned.1.call-update) | async-done | bytes 4194320 | tf_op jit(solution)/shard_map/all_gather | solution.py:37
  63.8 5.6 %all-to-all-start = ((bf16[256,2,4096]{0,2,1:T(8,128)(2,1)}), bf16[256,2,4096]{0,2,1:T(8,128)(2,1)}, u32[]{:S(2)}, u32[]{:S(2)}) async-start(bf16[256,2,4096]{0,2,1:T(8,128)(2,1)} %bitcast.34), calls=%async_computation | async-start | bytes 8388608 | tf_op jit(solution)/shard_map/all_to_all | solution.py:38
  69.5 0.3 collective-permute-start.2
  69.8 0.3 collective-permute-start.1
  70.0 0.0 copy-done.2
  70.0 53.0 %all_gather.7 = bf16[512,512]{1,0:T(8,128)(2,1)S(1)} all-gather(bf16[256,512]{1,0:T(8,128)(2,1)S(1)} %copy-done.2), channel_id=1, replica_groups=mesh['col'=16,'tok'=2] {'tok'}, dimensions={0}, use_global_device_ids=true | all-gather | bytes 786432 | tf_op jit(solution)/shard_map/all_gather | solution.py:39
  123.1 0.0 all-to-all-done
  123.1 6.3 %copy.18 = bf16[2,256,4096]{2,1,0:T(8,128)(2,1)} copy(bf16[2,256,4096]{1,2,0:T(8,128)(2,1)} %bitcast.1) | data formatting | bytes 8388608 | tf_op jit(solution)/shard_map/all_to_all | solution.py:38
  129.4 6.5 %convolution_convert_fusion = bf16[4096,512]{1,0:T(8,128)(2,1)} fusion(bf16[512,4096]{1,0:T(8,128)(2,1)} %bitcast.35, bf16[512,512]{1,0:T(8,128)(2,1)S(1)} %all_gather.7), kind=kOutput, calls=%fused_computation.6 | convolution fusion | flops 2149580800 | bytes 8912896 | tf_op jit(solution)/shard_map/dot_general | solution.py:40
  135.9 0.0 collective-permute-start
  135.9 0.0 copy-start.1
  135.9 4.5 %broadcast.17.clone.2 = bf16[4,1024,1024]{2,1,0:T(8,128)(2,1)} broadcast(bf16[]{:T(256)} %constant.17.clone.1), dimensions={} | broadcast | bytes 8388610 | tf_op jit(solution)/shard_map/broadcast.5
  140.4 0.0 copy-done.1
  140.4 0.0 copy-start
  140.4 2.6 constant_dynamic-update-slice_fusion.3
  143.0 0.0 slice-start
  143.0 4.3 %broadcast.17.clone.1 = bf16[4,1024,1024]{2,1,0:T(8,128)(2,1)} broadcast(bf16[]{:T(256)} %constant.17.clone.1), dimensions={} | broadcast | bytes 8388610 | tf_op jit(solution)/shard_map/broadcast.5
  147.3 0.0 copy-done
  147.3 0.0 slice-start.1
  147.3 0.0 slice-start.2
  147.3 2.6 constant_dynamic-update-slice_fusion.5
  149.9 0.0 slice-done
  149.9 1.1 slice-done.1
  151.0 0.0 slice-start.3
  151.0 4.5 %broadcast_multiply_fusion.1 = f32[4096,512]{1,0:T(8,128)} fusion(f32[4096,512]{1,0:T(8,128)S(1)} %bitcast.29), kind=kLoop, calls=%fused_computation.14 | loop fusion | flops 2097152 | bytes 16777216 | tf_op jit(solution)/shard_map/mul | solution.py:61
  155.5 0.0 slice-done.2
  155.5 0.0 slice-done.3
  155.5 4.5 %broadcast_multiply_fusion = f32[4096,512]{1,0:T(8,128)} fusion(f32[4096,512]{1,0:T(8,128)S(1)} %bitcast.31), kind=kLoop, calls=%fused_computation.9 | loop fusion | flops 2097152 | bytes 16777216 | tf_op jit(solution)/shard_map/mul | solution.py:63
  160.0 0.0 collective-permute-done.2
  160.0 4.6 %constant_dynamic-update-slice_fusion.2 = bf16[4,1024,1024]{2,1,0:T(8,128)(2,1)} fusion(bf16[4,1024,1024]{2,1,0:T(8,128)(2,1)} %constant_dynamic-update-slice_fusion.3, bf16[4,512,1024]{2,1,0:T(8,128)(2,1)} %collective-permute-done.2, s32[]{:T(128)S(6)} %select_n.30), kind=kLoop, calls=%fused_computation.21 | loop fusion | bytes 8388612 | tf_op jit(solution)/shard_map/dynamic_update_slice | solution.py:27
  164.6 0.0 collective-permute-done.1
  164.6 4.7 %constant_dynamic-update-slice_fusion.4 = bf16[4,1024,1024]{2,1,0:T(8,128)(2,1)} fusion(bf16[4,1024,1024]{2,1,0:T(8,128)(2,1)} %constant_dynamic-update-slice_fusion.5, bf16[4,512,1024]{2,1,0:T(8,128)(2,1)} %collective-permute-done.1, s32[]{:T(128)S(6)} %select_n.30), kind=kLoop, calls=%fused_computation.23 | loop fusion | bytes 8388612 | tf_op jit(solution)/shard_map/dynamic_update_slice | solution.py:27
  169.3 4.3 %broadcast.17.clone = bf16[4,1024,1024]{2,1,0:T(8,128)(2,1)} broadcast(bf16[]{:T(256)} %constant.17.clone.1), dimensions={} | broadcast | bytes 8388610 | tf_op jit(solution)/shard_map/broadcast.5
  173.6 4.6 %constant_dynamic-update-slice_fusion.7 = bf16[4,1024,1024]{2,1,0:T(8,128)(2,1)} fusion(bf16[4,1024,1024]{2,1,0:T(8,128)(2,1)} %broadcast.17.clone, bf16[4,1024,512]{2,1,0:T(8,128)(2,1)} %bitcast.3, s32[]{:T(128)S(6)} %select_n.29), kind=kLoop, calls=%fused_computation.27 | loop fusion | bytes 8388612 | tf_op jit(solution)/shard_map/dynamic_update_slice | solution.py:26
  178.2 0.0 collective-permute-done
  178.2 4.5 %constant_dynamic-update-slice_fusion.6 = bf16[4,1024,1024]{2,1,0:T(8,128)(2,1)} fusion(bf16[4,1024,1024]{2,1,0:T(8,128)(2,1)} %constant_dynamic-update-slice_fusion.7, bf16[4,1024,512]{2,1,0:T(8,128)(2,1)} %collective-permute-done, s32[]{:T(128)S(6)} %select_n.30), kind=kLoop, calls=%fused_computation.26 | loop fusion | bytes 8388612 | tf_op jit(solution)/shard_map/dynamic_update_slice | solution.py:27
  182.7 4.3 %broadcast.17 = bf16[4,1024,1024]{2,1,0:T(8,128)(2,1)} broadcast(bf16[]{:T(256)} %constant.17.clone.1), dimensions={} | broadcast | bytes 8388610 | tf_op jit(solution)/shard_map/broadcast.5
  187.0 29.9 %constant_dynamic-update-slice_fusion.1 = (bf16[4,1024,1024]{2,1,0:T(8,128)(2,1)}, bf16[4,1024,512]{2,1,0:T(8,128)(2,1)}, f32[4,1024,512]{2,1,0:T(8,128)}, f32[4,1024,512]{2,1,0:T(8,128)}) fusion(bf16[4,1024,1024]{2,1,0:T(8,128)(2,1)} %broadcast.17, s32[]{:T(128)S(6)} %select_n.29, f32[4,1024,512]{2,1,0:T(8,128)} %bitcast.33, f32[4,1024,512]{2,1,0:T(8,128)} %bitcast.32, ...), kind=kOutput, calls=%fused_computation.19 | convolution fusion | flops 8613003264 | bytes 62914568 | tf_op jit(solution)/shard_map/nab,nac->nbc/dot_general | solution.py:60
  216.9 0.4 collective-permute-start.3
  217.3 15.4 %multiply_add_fusion.2 = f32[4,512,1024]{2,1,0:T(8,128)} fusion(f32[4,512,1024]{2,1,0:T(8,128)} %param.10, bf16[4,1024,1024]{2,1,0:T(8,128)(2,1)} %constant_dynamic-update-slice_fusion.6, s32[]{:T(128)S(6)} %select_n.31), kind=kOutput, calls=%fused_computation.5 | convolution fusion | flops 4301258752 | bytes 29360132 | tf_op jit(solution)/shard_map/nab,ncb->nac/dot_general | solution.py:54
  232.8 15.3 %multiply_add_fusion.1 = f32[4,512,1024]{2,1,0:T(8,128)} fusion(f32[4,512,1024]{2,1,0:T(8,128)} %param.11, bf16[4,1024,512]{2,1,0:T(8,128)(2,1)} %bitcast.3, bf16[4,1024,1024]{2,1,0:T(8,128)(2,1)} %constant_dynamic-update-slice_fusion.6), kind=kOutput, calls=%fused_computation.4 | convolution fusion | flops 4301258752 | bytes 29360128 | tf_op jit(solution)/shard_map/nat,nab->ntb/dot_general | solution.py:57
  248.1 0.0 collective-permute-done.3
  248.1 4.5 %constant_dynamic-update-slice_fusion = bf16[4,1024,1024]{2,1,0:T(8,128)(2,1)} fusion(bf16[4,1024,1024]{2,1,0:T(8,128)(2,1)} %get-tuple-element.5, bf16[4,1024,512]{2,1,0:T(8,128)(2,1)} %collective-permute-done.3, s32[]{:T(128)S(6)} %select_n.30), kind=kLoop, calls=%fused_computation.18 | loop fusion | bytes 8388612 | tf_op jit(solution)/shard_map/dynamic_update_slice | solution.py:27
  252.6 14.5 %fusion.13 = bf16[4,1024,512]{2,1,0:T(8,128)(2,1)} fusion(bf16[4,1024,1024]{2,1,0:T(8,128)(2,1)} %constant_dynamic-update-slice_fusion.4, bf16[4,1024,1024]{2,1,0:T(8,128)(2,1)} %constant_dynamic-update-slice_fusion, bf16[4,512,1024]{2,1,0:T(8,128)(2,1)} %param.13), kind=kOutput, calls=%fused_computation.17 | convolution fusion | flops 8592031744 | bytes 25165824 | tf_op jit(solution)/shard_map/nab,nbc->nac/dot_general | solution.py:76
  (2 shorter events, 0.0 us)
Async XLA Ops:
  7.2 62.9 %copy-start.2 = (bf16[256,512]{1,0:T(8,128)(2,1)S(1)}, bf16[256,512]{1,0:T(8,128)(2,1)}, u32[]{:S(2)}) copy-start(bf16[256,512]{1,0:T(8,128)(2,1)} %param.9) | copy-start | bytes 786436
  7.2 56.7 %all-gather.2.cloned.1.call-start = ((), (), s32[]{:S(2)}) async-start(), calls=%async_computation.1 | async-start | bytes 4456448 | tf_op jit(solution)/shard_map/all_gather | solution.py:37
  63.8 59.2 %all-to-all-start = ((bf16[256,2,4096]{0,2,1:T(8,128)(2,1)}), bf16[256,2,4096]{0,2,1:T(8,128)(2,1)}, u32[]{:S(2)}, u32[]{:S(2)}) async-start(bf16[256,2,4096]{0,2,1:T(8,128)(2,1)} %bitcast.34), calls=%async_computation | async-start | bytes 8388608 | tf_op jit(solution)/shard_map/all_to_all | solution.py:38
  69.5 90.5 %collective-permute-start.2 = (bf16[4,512,1024]{2,1,0:T(8,128)(2,1)}, bf16[4,512,1024]{2,1,0:T(8,128)(2,1)}, u32[]{:S(2)}, u32[]{:S(2)}) collective-permute-start(bf16[4,512,1024]{2,1,0:T(8,128)(2,1)} %param.13), channel_id=1, source_target_pairs={{0,2},{2,0},{4,6},{6,4},{8,10},{10,8},{12,14},{14,12},{16,18},{18,... | collective-permute-start | bytes 12582920 | tf_op jit(solution)/shard_map/ppermute | solution.py:16
  69.8 94.8 %collective-permute-start.1 = (bf16[4,512,1024]{2,1,0:T(8,128)(2,1)}, bf16[4,512,1024]{2,1,0:T(8,128)(2,1)}, u32[]{:S(2)}, u32[]{:S(2)}) collective-permute-start(bf16[4,512,1024]{2,1,0:T(8,128)(2,1)} %param.12), channel_id=1, source_target_pairs={{0,2},{2,0},{4,6},{6,4},{8,10},{10,8},{12,14},{14,12},{16,18},{18,... | collective-permute-start | bytes 12582920 | tf_op jit(solution)/shard_map/ppermute | solution.py:16
  135.9 42.3 %collective-permute-start = (bf16[4,1024,512]{2,1,0:T(8,128)(2,1)}, bf16[4,1024,512]{2,1,0:T(8,128)(2,1)}, u32[]{:S(2)}, u32[]{:S(2)}) collective-permute-start(bf16[4,1024,512]{2,1,0:T(8,128)(2,1)} %bitcast.3), channel_id=1, source_target_pairs={{0,2},{2,0},{4,6},{6,4},{8,10},{10,8},{12,14},{14,12},{16,18},{18,... | collective-permute-start | bytes 12582920 | tf_op jit(solution)/shard_map/ppermute | solution.py:16
  135.9 4.5 %copy-start.1 = (bf16[4,512,1024]{2,1,0:T(8,128)(2,1)S(1)}, bf16[4,512,1024]{2,1,0:T(8,128)(2,1)}, u32[]{:S(2)}) copy-start(bf16[4,512,1024]{2,1,0:T(8,128)(2,1)} %param.13) | copy-start | bytes 12582916
  140.4 6.9 %copy-start = (bf16[4,512,1024]{2,1,0:T(8,128)(2,1)S(1)}, bf16[4,512,1024]{2,1,0:T(8,128)(2,1)}, u32[]{:S(2)}) copy-start(bf16[4,512,1024]{2,1,0:T(8,128)(2,1)} %param.12) | copy-start | bytes 12582916
  143.0 6.9 %slice-start = ((s8[8388608]{0:T(1024)(128)(4,1)}), s8[4194304]{0:T(1024)(128)(4,1)S(1)}, s32[]{:S(2)}) async-start(s8[8388608]{0:T(1024)(128)(4,1)} %bitcast.28), calls=%async_computation.2 | async-start | bytes 8388608
  147.3 3.7 %slice-start.1 = ((s8[8388608]{0:T(1024)(128)(4,1)}), s8[4194304]{0:T(1024)(128)(4,1)S(1)}, s32[]{:S(2)}) async-start(s8[8388608]{0:T(1024)(128)(4,1)} %bitcast.28), calls=%async_computation.3 | async-start | bytes 8388608
  147.3 8.2 %slice-start.2 = ((s8[8388608]{0:T(1024)(128)(4,1)}), s8[4194304]{0:T(1024)(128)(4,1)S(1)}, s32[]{:S(2)}) async-start(s8[8388608]{0:T(1024)(128)(4,1)} %bitcast.30), calls=%async_computation.4 | async-start | bytes 8388608
  151.0 4.5 %slice-start.3 = ((s8[8388608]{0:T(1024)(128)(4,1)}), s8[4194304]{0:T(1024)(128)(4,1)S(1)}, s32[]{:S(2)}) async-start(s8[8388608]{0:T(1024)(128)(4,1)} %bitcast.30), calls=%async_computation.5 | async-start | bytes 8388608
  216.9 31.2 %collective-permute-start.3 = (bf16[4,1024,512]{2,1,0:T(8,128)(2,1)}, bf16[4,1024,512]{2,1,0:T(8,128)(2,1)}, u32[]{:S(2)}, u32[]{:S(2)}) collective-permute-start(bf16[4,1024,512]{2,1,0:T(8,128)(2,1)} %get-tuple-element.6), channel_id=1, source_target_pairs={{0,2},{2,0},{4,6},{6,4},{8,10},{10,8},{12,14},{14,12},{16,18},{18,... | collective-permute-start | bytes 12582920 | tf_op jit(solution)/shard_map/ppermute | solution.py:16
Sparse Core Ops, SparseCore 0:
  10.7 53.0 all-gather.1
where the time goes:
time: 274 us
  matrix products  81.7 us (30%)
  waiting for transfers between devices  54.8 us (20%)
  local copies, waits for them, and re-layouts  54.7 us (20%)
  blocking collectives  53 us (19%)
  between operations  14.1 us (5%)
  other arithmetic  8.98 us (3%)
  starting transfers between devices  6.68 us (2%)
    all_gather x1, waiting for transfers between devices, shards(): whole = lax.all_gather(acts, 'col', axis=1, tiled=True)  54.8 us
    all_gather x1, blocking collectives, shards(): all_grads = lax.all_gather(grad_out, 'tok', axis=0, tiled=True)  53 us
    dot_general x1, matrix products, shards(): jnp.einsum('nab,nac->nbc', left_full, mixed, preferred_element_type=jnp.f...  29.9 us
    dynamic_update_slice x4, local copies, waits for them, and re-layouts, join_pair(): return lax.dynamic_update_slice_in_dim(joined, incoming, theirs_at, axis)  18.3 us
    another operation x4, local copies, waits for them, and re-layouts  17.4 us
    dot_general x1, matrix products, shards(): jnp.einsum('nab,ncb->nac', lead, tiles, preferred_element_type=jnp.float32)  15.4 us
    dot_general x1, matrix products, shards(): jnp.einsum('nat,nab->ntb', own, tiles, preferred_element_type=jnp.float32)  15.3 us
    dot_general x1, matrix products, shards(): jnp.einsum('nab,nbc->nac', left_full, back, preferred_element_type=jnp.fl...  14.5 us
  transfers between devices with their start and end apart: 6, of which 1 were waited for; matrix products, arithmetic and copies ran while one was open for 31% of the time, Pallas kernels for 0%

commit v1 on v0

--- a/solution.py
+++ b/solution.py
@@ -10,6 +10,16 @@
 first_corr = 1.0 - 0.9**4
 second_corr = 1.0 - 0.95**4
 epsilon = 1e-08
+
+
+def gather_by_hops(block, axis, dim):
+    size = lax.axis_size(axis)
+    held, blocks = (block, [block])
+    for _ in range(size - 1):
+        held = lax.ppermute(held, axis, [(i, (i + 1) % size) for i in range(size)])
+        blocks.insert(0, held)
+    merged = jnp.concatenate(blocks, axis=dim)
+    return jnp.roll(merged, (lax.axis_index(axis) + 1) * block.shape[dim], axis=dim)
 
 
 def swapped(array, axis, distance):
@@ -34,7 +44,7 @@
     nbits = groups.bit_length() - 1
     member = lax.axis_index("col") % groups
     contract = (((0,), (0,)), ((), ()))
-    whole = lax.all_gather(acts, "col", axis=1, tiled=True)
+    whole = gather_by_hops(acts, "col", 1)
     block_rows = lax.all_to_all(whole, "tok", split_axis=1, concat_axis=0, tiled=True)
     all_grads = lax.all_gather(grad_out, "tok", axis=0, tiled=True)
     grad = lax.dot_general(block_rows, all_grads, contract, preferred_element_type=jnp.float32)

time: 274 us -> 337 us (1.23)
  waiting for transfers between devices: 54.8 us -> 128 us
  between operations: 14.1 us -> 0.94 us
  local copies, waits for them, and re-layouts: 54.7 us -> 62.5 us
  blocking collectives: 53 us -> 46.1 us
    ppermute x0 -> x15, waiting for transfers between devices: none -> 128 us  [gather_by_hops(): held = lax.ppermute(held, axis, [(i, (i + 1) % size) for i in range(size)])]
    all_gather x1 -> x0, waiting for transfers between devices: 54.8 us -> none  [shards(): whole = lax.all_gather(acts, 'col', axis=1, tiled=True)]
    all_gather x1, blocking collectives: 53 us -> 46.1 us  [shards(): all_grads = lax.all_gather(grad_out, 'tok', axis=0, tiled=True)]
    unnamed x15 -> x50, local copies, waits for them, and re-layouts: 2.97 us -> 8.28 us
  transfers between devices with their start and end apart: 6 -> 20, of which waited for: 1 -> 15; matrix products, arithmetic and copies ran while one was open for 31% -> 25% of each run, Pallas kernels for 0% -> 0%
where the time goes in v1:
time: 337 us; the launch traced here: 336 us
  waiting for transfers between devices  128 us (38%)
  matrix products  81.7 us (24%)
  local copies, waits for them, and re-layouts  62.5 us (19%)
  blocking collectives  46.1 us (14%)
  other arithmetic  8.98 us (3%)
  starting transfers between devices  7.25 us (2%)
    ppermute x15, waiting for transfers between devices, gather_by_hops(): held = lax.ppermute(held, axis, [(i, (i + 1) % size) for i in range(size)])  128 us
    all_gather x1, blocking collectives, shards(): all_grads = lax.all_gather(grad_out, 'tok', axis=0, tiled=True)  46.1 us
    dot_general x1, matrix products, shards(): jnp.einsum('nab,nac->nbc', left_full, mixed, preferred_element_type=jnp.f...  29.9 us
    dynamic_update_slice x4, local copies, waits for them, and re-layouts, join_pair(): return lax.dynamic_update_slice_in_dim(joined, incoming, theirs_at, axis)  18.4 us
    another operation x4, local copies, waits for them, and re-layouts  17.5 us
    dot_general x1, matrix products, shards(): jnp.einsum('nab,ncb->nac', lead, tiles, preferred_element_type=jnp.float32)  15.4 us
    dot_general x1, matrix products, shards(): jnp.einsum('nat,nab->ntb', own, tiles, preferred_element_type=jnp.float32)  15.3 us
    dot_general x1, matrix products, shards(): jnp.einsum('nab,nbc->nac', left_full, back, preferred_element_type=jnp.fl...  14.5 us
  transfers between devices with their start and end apart: 20, of which 15 were waited for; matrix products, arithmetic and copies ran while one was open for 25% of the time, Pallas kernels for 0%

profile of v1, /device:TPU:0, one launch (start us, length us, event | category | flops | bytes accessed | tf_op | source)
XLA Modules:
  0.0 335.8 jit_solution(12581350725638169202)
XLA Ops:
  0.6 1.1 copy.17
  1.7 0.5 collective-permute-start
  2.3 9.0 %collective-permute-done = bf16[256,512]{0,1:T(8,128)(2,1)S(1)} collective-permute-done((bf16[256,512]{0,1:T(8,128)(2,1)S(1)}, bf16[256,512]{0,1:T(8,128)(2,1)S(1)}, u32[]{:S(2)}, u32[]{:S(2)}) %collective-permute-start) | collective-permute-done | bytes 262176 | tf_op jit(solution)/shard_map/ppermute | solution.py:19
  11.3 0.0 collective-permute-start.1
  11.3 8.5 %collective-permute-done.1 = bf16[256,512]{0,1:T(8,128)(2,1)S(1)} collective-permute-done((bf16[256,512]{0,1:T(8,128)(2,1)S(1)}, bf16[256,512]{0,1:T(8,128)(2,1)S(1)}, u32[]{:S(2)}, u32[]{:S(2)}) %collective-permute-start.1) | collective-permute-done | bytes 262176 | tf_op jit(solution)/shard_map/ppermute | solution.py:19
  19.8 0.0 collective-permute-start.2
  19.8 8.5 %collective-permute-done.2 = bf16[256,512]{0,1:T(8,128)(2,1)S(1)} collective-permute-done((bf16[256,512]{0,1:T(8,128)(2,1)S(1)}, bf16[256,512]{0,1:T(8,128)(2,1)S(1)}, u32[]{:S(2)}, u32[]{:S(2)}) %collective-permute-start.2) | collective-permute-done | bytes 262176 | tf_op jit(solution)/shard_map/ppermute | solution.py:19
  28.3 0.0 collective-permute-start.3
  28.3 8.5 %collective-permute-done.3 = bf16[256,512]{0,1:T(8,128)(2,1)S(1)} collective-permute-done((bf16[256,512]{0,1:T(8,128)(2,1)S(1)}, bf16[256,512]{0,1:T(8,128)(2,1)S(1)}, u32[]{:S(2)}, u32[]{:S(2)}) %collective-permute-start.3) | collective-permute-done | bytes 262176 | tf_op jit(solution)/shard_map/ppermute | solution.py:19
  36.8 0.0 collective-permute-start.4
  36.8 8.5 %collective-permute-done.4 = bf16[256,512]{0,1:T(8,128)(2,1)S(1)} collective-permute-done((bf16[256,512]{0,1:T(8,128)(2,1)S(1)}, bf16[256,512]{0,1:T(8,128)(2,1)S(1)}, u32[]{:S(2)}, u32[]{:S(2)}) %collective-permute-start.4) | collective-permute-done | bytes 262176 | tf_op jit(solution)/shard_map/ppermute | solution.py:19
  45.3 8.5 %collective-permute-done.5 = bf16[256,512]{0,1:T(8,128)(2,1)S(1)} collective-permute-done((bf16[256,512]{0,1:T(8,128)(2,1)S(1)}, bf16[256,512]{0,1:T(8,128)(2,1)S(1)}, u32[]{:S(2)}, u32[]{:S(2)}) %collective-permute-start.5) | collective-permute-done | bytes 262176 | tf_op jit(solution)/shard_map/ppermute | solution.py:19
  53.7 0.0 collective-permute-start.6
  53.8 8.5 %collective-permute-done.6 = bf16[256,512]{0,1:T(8,128)(2,1)S(1)} collective-permute-done((bf16[256,512]{0,1:T(8,128)(2,1)S(1)}, bf16[256,512]{0,1:T(8,128)(2,1)S(1)}, u32[]{:S(2)}, u32[]{:S(2)}) %collective-permute-start.6) | collective-permute-done | bytes 262176 | tf_op jit(solution)/shard_map/ppermute | solution.py:19
  62.2 0.0 collective-permute-start.7
  62.2 8.5 %collective-permute-done.7 = bf16[256,512]{0,1:T(8,128)(2,1)S(1)} collective-permute-done((bf16[256,512]{0,1:T(8,128)(2,1)S(1)}, bf16[256,512]{0,1:T(8,128)(2,1)S(1)}, u32[]{:S(2)}, u32[]{:S(2)}) %collective-permute-start.7) | collective-permute-done | bytes 262176 | tf_op jit(solution)/shard_map/ppermute | solution.py:19
  70.7 0.0 collective-permute-start.8
  70.7 8.5 %collective-permute-done.8 = bf16[256,512]{0,1:T(8,128)(2,1)S(1)} collective-permute-done((bf16[256,512]{0,1:T(8,128)(2,1)S(1)}, bf16[256,512]{0,1:T(8,128)(2,1)S(1)}, u32[]{:S(2)}, u32[]{:S(2)}) %collective-permute-start.8) | collective-permute-done | bytes 262176 | tf_op jit(solution)/shard_map/ppermute | solution.py:19
  79.2 0.0 collective-permute-start.9
  79.2 8.5 %collective-permute-done.9 = bf16[256,512]{0,1:T(8,128)(2,1)S(1)} collective-permute-done((bf16[256,512]{0,1:T(8,128)(2,1)S(1)}, bf16[256,512]{0,1:T(8,128)(2,1)S(1)}, u32[]{:S(2)}, u32[]{:S(2)}) %collective-permute-start.9) | collective-permute-done | bytes 262176 | tf_op jit(solution)/shard_map/ppermute | solution.py:19
  87.7 8.5 %collective-permute-done.10 = bf16[256,512]{0,1:T(8,128)(2,1)S(1)} collective-permute-done((bf16[256,512]{0,1:T(8,128)(2,1)S(1)}, bf16[256,512]{0,1:T(8,128)(2,1)S(1)}, u32[]{:S(2)}, u32[]{:S(2)}) %collective-permute-start.10) | collective-permute-done | bytes 262176 | tf_op jit(solution)/shard_map/ppermute | solution.py:19
  96.2 8.5 %collective-permute-done.11 = bf16[256,512]{0,1:T(8,128)(2,1)S(1)} collective-permute-done((bf16[256,512]{0,1:T(8,128)(2,1)S(1)}, bf16[256,512]{0,1:T(8,128)(2,1)S(1)}, u32[]{:S(2)}, u32[]{:S(2)}) %collective-permute-start.11) | collective-permute-done | bytes 262176 | tf_op jit(solution)/shard_map/ppermute | solution.py:19
  104.7 8.5 %collective-permute-done.12 = bf16[256,512]{0,1:T(8,128)(2,1)S(1)} collective-permute-done((bf16[256,512]{0,1:T(8,128)(2,1)S(1)}, bf16[256,512]{0,1:T(8,128)(2,1)S(1)}, u32[]{:S(2)}, u32[]{:S(2)}) %collective-permute-start.12) | collective-permute-done | bytes 262176 | tf_op jit(solution)/shard_map/ppermute | solution.py:19
  113.2 0.7 copy-done.2
  113.9 0.0 collective-permute-start.13
  113.9 8.6 %collective-permute-done.13 = bf16[256,512]{0,1:T(8,128)(2,1)} collective-permute-done((bf16[256,512]{0,1:T(8,128)(2,1)S(1)}, bf16[256,512]{0,1:T(8,128)(2,1)}, u32[]{:S(2)}, u32[]{:S(2)}) %collective-permute-start.13) | collective-permute-done | bytes 262176 | tf_op jit(solution)/shard_map/ppermute | solution.py:19
  122.5 0.0 collective-permute-start.14
  122.5 8.8 %collective-permute-done.14 = bf16[256,512]{0,1:T(8,128)(2,1)} collective-permute-done((bf16[256,512]{0,1:T(8,128)(2,1)}, bf16[256,512]{0,1:T(8,128)(2,1)}, u32[]{:S(2)}, u32[]{:S(2)}) %collective-permute-start.14) | collective-permute-done | bytes 262176 | tf_op jit(solution)/shard_map/ppermute | solution.py:19
  131.3 1.0 constant_dynamic-update-slice_fusion.31
  132.3 1.0 constant_dynamic-update-slice_fusion.30
  133.3 1.0 constant_dynamic-update-slice_fusion.29
  134.6 1.0 constant_dynamic-update-slice_fusion.15
  135.6 1.0 constant_dynamic-update-slice_fusion.14
  136.9 0.0 copy-start.4
  136.9 2.3 constant_dynamic-slice_fusion
  139.2 5.6 %all-to-all-start = ((bf16[256,2,4096]{0,2,1:T(8,128)(2,1)}), bf16[256,2,4096]{0,2,1:T(8,128)(2,1)}, u32[]{:S(2)}, u32[]{:S(2)}) async-start(bf16[256,2,4096]{0,2,1:T(8,128)(2,1)} %bitcast.28), calls=%async_computation | async-start | bytes 8388608 | tf_op jit(solution)/shard_map/all_to_all | solution.py:48
  144.9 0.1 collective-permute-start.17
  145.0 0.5 collective-permute-start.16
  145.5 46.1 %all_gather.3 = bf16[512,512]{1,0:T(8,128)(2,1)S(1)} all-gather(bf16[256,512]{1,0:T(8,128)(2,1)S(1)} %copy-done.4), channel_id=1, replica_groups=mesh['col'=16,'tok'=2] {'tok'}, dimensions={0}, use_global_device_ids=true | all-gather | bytes 786432 | tf_op jit(solution)/shard_map/all_gather | solution.py:49
  191.6 0.0 all-to-all-done
  191.6 6.3 %copy.20 = bf16[2,256,4096]{2,1,0:T(8,128)(2,1)} copy(bf16[2,256,4096]{1,2,0:T(8,128)(2,1)} %bitcast.1) | data formatting | bytes 8388608 | tf_op jit(solution)/shard_map/all_to_all | solution.py:48
  197.9 6.6 %convolution_convert_fusion = bf16[4096,512]{1,0:T(8,128)(2,1)} fusion(bf16[512,4096]{1,0:T(8,128)(2,1)} %bitcast.35, bf16[512,512]{1,0:T(8,128)(2,1)S(1)} %all_gather.3), kind=kOutput, calls=%fused_computation.6 | convolution fusion | flops 2149580800 | bytes 8912896 | tf_op jit(solution)/shard_map/dot_general | solution.py:50
  204.5 4.5 %broadcast.18.clone.2 = bf16[4,1024,1024]{2,1,0:T(8,128)(2,1)} broadcast(bf16[]{:T(256)} %constant.51.clone.1), dimensions={} | broadcast | bytes 8388610 | tf_op jit(solution)/shard_map/broadcast.5
  208.9 2.6 constant_dynamic-update-slice_fusion.35
  211.5 4.3 %broadcast.18.clone.1 = bf16[4,1024,1024]{2,1,0:T(8,128)(2,1)} broadcast(bf16[]{:T(256)} %constant.51.clone.1), dimensions={} | broadcast | bytes 8388610 | tf_op jit(solution)/shard_map/broadcast.5
  215.9 2.6 constant_dynamic-update-slice_fusion.37
  218.4 1.1 slice-done.1
  219.6 4.5 %broadcast_multiply_fusion.1 = f32[4096,512]{1,0:T(8,128)} fusion(f32[4096,512]{1,0:T(8,128)S(1)} %bitcast.30), kind=kLoop, calls=%fused_computation.14 | loop fusion | flops 2097152 | bytes 16777216 | tf_op jit(solution)/shard_map/mul | solution.py:71
  224.1 4.5 %broadcast_multiply_fusion = f32[4096,512]{1,0:T(8,128)} fusion(f32[4096,512]{1,0:T(8,128)S(1)} %bitcast.32), kind=kLoop, calls=%fused_computation.9 | loop fusion | flops 2097152 | bytes 16777216 | tf_op jit(solution)/shard_map/mul | solution.py:73
  228.6 4.6 %constant_dynamic-update-slice_fusion.34 = bf16[4,1024,1024]{2,1,0:T(8,128)(2,1)} fusion(bf16[4,1024,1024]{2,1,0:T(8,128)(2,1)} %constant_dynamic-update-slice_fusion.35, bf16[4,512,1024]{2,1,0:T(8,128)(2,1)} %collective-permute-done.17, s32[]{:T(128)S(6)} %select_n.44), kind=kLoop, calls=%fused_computation.53 | loop fusion | bytes 8388612 | tf_op jit(solution)/shard_map/dynamic_update_slice | solution.py:37
  233.2 0.0 collective-permute-done.16
  233.2 4.7 %constant_dynamic-update-slice_fusion.36 = bf16[4,1024,1024]{2,1,0:T(8,128)(2,1)} fusion(bf16[4,1024,1024]{2,1,0:T(8,128)(2,1)} %constant_dynamic-update-slice_fusion.37, bf16[4,512,1024]{2,1,0:T(8,128)(2,1)} %collective-permute-done.16, s32[]{:T(128)S(6)} %select_n.44), kind=kLoop, calls=%fused_computation.55 | loop fusion | bytes 8388612 | tf_op jit(solution)/shard_map/dynamic_update_slice | solution.py:37
  237.9 4.3 %broadcast.18.clone = bf16[4,1024,1024]{2,1,0:T(8,128)(2,1)} broadcast(bf16[]{:T(256)} %constant.51.clone.1), dimensions={} | broadcast | bytes 8388610 | tf_op jit(solution)/shard_map/broadcast.5
  242.2 4.6 %constant_dynamic-update-slice_fusion.39 = bf16[4,1024,1024]{2,1,0:T(8,128)(2,1)} fusion(bf16[4,1024,1024]{2,1,0:T(8,128)(2,1)} %broadcast.18.clone, bf16[4,1024,512]{2,1,0:T(8,128)(2,1)} %bitcast.3, s32[]{:T(128)S(6)} %select_n.43), kind=kLoop, calls=%fused_computation.59 | loop fusion | bytes 8388612 | tf_op jit(solution)/shard_map/dynamic_update_slice | solution.py:36
  246.8 0.0 collective-permute-done.15
  246.8 4.6 %constant_dynamic-update-slice_fusion.38 = bf16[4,1024,1024]{2,1,0:T(8,128)(2,1)} fusion(bf16[4,1024,1024]{2,1,0:T(8,128)(2,1)} %constant_dynamic-update-slice_fusion.39, bf16[4,1024,512]{2,1,0:T(8,128)(2,1)} %collective-permute-done.15, s32[]{:T(128)S(6)} %select_n.44), kind=kLoop, calls=%fused_computation.58 | loop fusion | bytes 8388612 | tf_op jit(solution)/shard_map/dynamic_update_slice | solution.py:37
  251.4 4.3 %broadcast.18 = bf16[4,1024,1024]{2,1,0:T(8,128)(2,1)} broadcast(bf16[]{:T(256)} %constant.51.clone.1), dimensions={} | broadcast | bytes 8388610 | tf_op jit(solution)/shard_map/broadcast.5
  255.7 29.9 %constant_dynamic-update-slice_fusion.33 = (bf16[4,1024,1024]{2,1,0:T(8,128)(2,1)}, bf16[4,1024,512]{2,1,0:T(8,128)(2,1)}, f32[4,1024,512]{2,1,0:T(8,128)}, f32[4,1024,512]{2,1,0:T(8,128)}) fusion(bf16[4,1024,1024]{2,1,0:T(8,128)(2,1)} %broadcast.18, s32[]{:T(128)S(6)} %select_n.43, f32[4,1024,512]{2,1,0:T(8,128)} %bitcast.34, ...), kind=kOutput, calls=%fused_computation.51 | convolution fusion | flops 8613003264 | bytes 62914568 | tf_op jit(solution)/shard_map/nab,nac->nbc/dot_general | solution.py:70
  285.6 0.5 collective-permute-start.18
  286.1 15.4 %multiply_add_fusion.2 = f32[4,512,1024]{2,1,0:T(8,128)} fusion(f32[4,512,1024]{2,1,0:T(8,128)} %param.10, bf16[4,1024,1024]{2,1,0:T(8,128)(2,1)} %constant_dynamic-update-slice_fusion.38, s32[]{:T(128)S(6)} %select_n.45), kind=kOutput, calls=%fused_computation.5 | convolution fusion | flops 4301258752 | bytes 29360132 | tf_op jit(solution)/shard_map/nab,ncb->nac/dot_general | solution.py:64
  301.5 15.3 %multiply_add_fusion.1 = f32[4,512,1024]{2,1,0:T(8,128)} fusion(f32[4,512,1024]{2,1,0:T(8,128)} %param.11, bf16[4,1024,512]{2,1,0:T(8,128)(2,1)} %bitcast.3, bf16[4,1024,1024]{2,1,0:T(8,128)(2,1)} %constant_dynamic-update-slice_fusion.38), kind=kOutput, calls=%fused_computation.4 | convolution fusion | flops 4301258752 | bytes 29360128 | tf_op jit(solution)/shard_map/nat,nab->ntb/dot_general | solution.py:67
  316.9 0.0 collective-permute-done.18
  316.9 4.5 %constant_dynamic-update-slice_fusion.32 = bf16[4,1024,1024]{2,1,0:T(8,128)(2,1)} fusion(bf16[4,1024,1024]{2,1,0:T(8,128)(2,1)} %get-tuple-element.5, bf16[4,1024,512]{2,1,0:T(8,128)(2,1)} %collective-permute-done.18, s32[]{:T(128)S(6)} %select_n.44), kind=kLoop, calls=%fused_computation.50 | loop fusion | bytes 8388612 | tf_op jit(solution)/shard_map/dynamic_update_slice | solution.py:37
  321.3 14.5 %fusion.13 = bf16[4,1024,512]{2,1,0:T(8,128)(2,1)} fusion(bf16[4,1024,1024]{2,1,0:T(8,128)(2,1)} %constant_dynamic-update-slice_fusion.36, bf16[4,1024,1024]{2,1,0:T(8,128)(2,1)} %constant_dynamic-update-slice_fusion.32, bf16[4,512,1024]{2,1,0:T(8,128)(2,1)} %param.13), kind=kOutput, calls=%fused_computation.17 | convolution fusion | flops 8592031744 | bytes 25165824 | tf_op jit(solution)/shard_map/nab,nbc->nac/dot_general | solution.py:86
  (50 shorter events, 0.6 us)
Async XLA Ops:
  1.7 9.6 %collective-permute-start = (bf16[256,512]{0,1:T(8,128)(2,1)S(1)}, bf16[256,512]{0,1:T(8,128)(2,1)S(1)}, u32[]{:S(2)}, u32[]{:S(2)}) collective-permute-start(bf16[256,512]{0,1:T(8,128)(2,1)S(1)} %copy.17), channel_id=1, source_target_pairs={{0,2},{2,4},{4,6},{6,8},{8,10},{10,12},{12,14},{14,16},{16,18},{18... | collective-permute-start | bytes 786440 | tf_op jit(solution)/shard_map/ppermute | solution.py:19
  11.3 8.5 %collective-permute-start.1 = (bf16[256,512]{0,1:T(8,128)(2,1)S(1)}, bf16[256,512]{0,1:T(8,128)(2,1)S(1)}, u32[]{:S(2)}, u32[]{:S(2)}) collective-permute-start(bf16[256,512]{0,1:T(8,128)(2,1)S(1)} %collective-permute-done), channel_id=1, source_target_pairs={{0,2},{2,4},{4,6},{6,8},{8,10},{10,12},{12,14},{14,16},{16,18},{18... | collective-permute-start | bytes 786440 | tf_op jit(solution)/shard_map/ppermute | solution.py:19
  19.8 8.5 %collective-permute-start.2 = (bf16[256,512]{0,1:T(8,128)(2,1)S(1)}, bf16[256,512]{0,1:T(8,128)(2,1)S(1)}, u32[]{:S(2)}, u32[]{:S(2)}) collective-permute-start(bf16[256,512]{0,1:T(8,128)(2,1)S(1)} %collective-permute-done.1), channel_id=1, source_target_pairs={{0,2},{2,4},{4,6},{6,8},{8,10},{10,12},{12,14},{14,16},{16,18},{18... | collective-permute-start | bytes 786440 | tf_op jit(solution)/shard_map/ppermute | solution.py:19
  28.3 8.5 %collective-permute-start.3 = (bf16[256,512]{0,1:T(8,128)(2,1)S(1)}, bf16[256,512]{0,1:T(8,128)(2,1)S(1)}, u32[]{:S(2)}, u32[]{:S(2)}) collective-permute-start(bf16[256,512]{0,1:T(8,128)(2,1)S(1)} %collective-permute-done.2), channel_id=1, source_target_pairs={{0,2},{2,4},{4,6},{6,8},{8,10},{10,12},{12,14},{14,16},{16,18},{18... | collective-permute-start | bytes 786440 | tf_op jit(solution)/shard_map/ppermute | solution.py:19
  36.8 8.5 %collective-permute-start.4 = (bf16[256,512]{0,1:T(8,128)(2,1)S(1)}, bf16[256,512]{0,1:T(8,128)(2,1)S(1)}, u32[]{:S(2)}, u32[]{:S(2)}) collective-permute-start(bf16[256,512]{0,1:T(8,128)(2,1)S(1)} %collective-permute-done.3), channel_id=1, source_target_pairs={{0,2},{2,4},{4,6},{6,8},{8,10},{10,12},{12,14},{14,16},{16,18},{18... | collective-permute-start | bytes 786440 | tf_op jit(solution)/shard_map/ppermute | solution.py:19
  45.3 8.5 %collective-permute-start.5 = (bf16[256,512]{0,1:T(8,128)(2,1)S(1)}, bf16[256,512]{0,1:T(8,128)(2,1)S(1)}, u32[]{:S(2)}, u32[]{:S(2)}) collective-permute-start(bf16[256,512]{0,1:T(8,128)(2,1)S(1)} %collective-permute-done.4), channel_id=1, source_target_pairs={{0,2},{2,4},{4,6},{6,8},{8,10},{10,12},{12,14},{14,16},{16,18},{18... | collective-permute-start | bytes 786440 | tf_op jit(solution)/shard_map/ppermute | solution.py:19
  53.7 8.5 %collective-permute-start.6 = (bf16[256,512]{0,1:T(8,128)(2,1)S(1)}, bf16[256,512]{0,1:T(8,128)(2,1)S(1)}, u32[]{:S(2)}, u32[]{:S(2)}) collective-permute-start(bf16[256,512]{0,1:T(8,128)(2,1)S(1)} %collective-permute-done.5), channel_id=1, source_target_pairs={{0,2},{2,4},{4,6},{6,8},{8,10},{10,12},{12,14},{14,16},{16,18},{18... | collective-permute-start | bytes 786440 | tf_op jit(solution)/shard_map/ppermute | solution.py:19
  62.2 8.5 %collective-permute-start.7 = (bf16[256,512]{0,1:T(8,128)(2,1)S(1)}, bf16[256,512]{0,1:T(8,128)(2,1)S(1)}, u32[]{:S(2)}, u32[]{:S(2)}) collective-permute-start(bf16[256,512]{0,1:T(8,128)(2,1)S(1)} %collective-permute-done.6), channel_id=1, source_target_pairs={{0,2},{2,4},{4,6},{6,8},{8,10},{10,12},{12,14},{14,16},{16,18},{18... | collective-permute-start | bytes 786440 | tf_op jit(solution)/shard_map/ppermute | solution.py:19
  70.7 8.5 %collective-permute-start.8 = (bf16[256,512]{0,1:T(8,128)(2,1)S(1)}, bf16[256,512]{0,1:T(8,128)(2,1)S(1)}, u32[]{:S(2)}, u32[]{:S(2)}) collective-permute-start(bf16[256,512]{0,1:T(8,128)(2,1)S(1)} %collective-permute-done.7), channel_id=1, source_target_pairs={{0,2},{2,4},{4,6},{6,8},{8,10},{10,12},{12,14},{14,16},{16,18},{18... | collective-permute-start | bytes 786440 | tf_op jit(solution)/shard_map/ppermute | solution.py:19
  79.2 8.5 %collective-permute-start.9 = (bf16[256,512]{0,1:T(8,128)(2,1)S(1)}, bf16[256,512]{0,1:T(8,128)(2,1)S(1)}, u32[]{:S(2)}, u32[]{:S(2)}) collective-permute-start(bf16[256,512]{0,1:T(8,128)(2,1)S(1)} %collective-permute-done.8), channel_id=1, source_target_pairs={{0,2},{2,4},{4,6},{6,8},{8,10},{10,12},{12,14},{14,16},{16,18},{18... | collective-permute-start | bytes 786440 | tf_op jit(solution)/shard_map/ppermute | solution.py:19
  87.7 8.5 %collective-permute-start.10 = (bf16[256,512]{0,1:T(8,128)(2,1)S(1)}, bf16[256,512]{0,1:T(8,128)(2,1)S(1)}, u32[]{:S(2)}, u32[]{:S(2)}) collective-permute-start(bf16[256,512]{0,1:T(8,128)(2,1)S(1)} %collective-permute-done.9), channel_id=1, source_target_pairs={{0,2},{2,4},{4,6},{6,8},{8,10},{10,12},{12,14},{14,16},{16,18},{18... | collective-permute-start | bytes 786440 | tf_op jit(solution)/shard_map/ppermute | solution.py:19
  96.2 8.5 %collective-permute-start.11 = (bf16[256,512]{0,1:T(8,128)(2,1)S(1)}, bf16[256,512]{0,1:T(8,128)(2,1)S(1)}, u32[]{:S(2)}, u32[]{:S(2)}) collective-permute-start(bf16[256,512]{0,1:T(8,128)(2,1)S(1)} %collective-permute-done.10), channel_id=1, source_target_pairs={{0,2},{2,4},{4,6},{6,8},{8,10},{10,12},{12,14},{14,16},{16,18},{18... | collective-permute-start | bytes 786440 | tf_op jit(solution)/shard_map/ppermute | solution.py:19
  104.7 8.5 %collective-permute-start.12 = (bf16[256,512]{0,1:T(8,128)(2,1)S(1)}, bf16[256,512]{0,1:T(8,128)(2,1)S(1)}, u32[]{:S(2)}, u32[]{:S(2)}) collective-permute-start(bf16[256,512]{0,1:T(8,128)(2,1)S(1)} %collective-permute-done.11), channel_id=1, source_target_pairs={{0,2},{2,4},{4,6},{6,8},{8,10},{10,12},{12,14},{14,16},{16,18},{18... | collective-permute-start | bytes 786440 | tf_op jit(solution)/shard_map/ppermute | solution.py:19
  113.2 0.7 copy-start.2
  113.9 8.6 %collective-permute-start.13 = (bf16[256,512]{0,1:T(8,128)(2,1)S(1)}, bf16[256,512]{0,1:T(8,128)(2,1)}, u32[]{:S(2)}, u32[]{:S(2)}) collective-permute-start(bf16[256,512]{0,1:T(8,128)(2,1)S(1)} %collective-permute-done.12), channel_id=1, source_target_pairs={{0,2},{2,4},{4,6},{6,8},{8,10},{10,12},{12,14},{14,16},{16,18},{18... | collective-permute-start | bytes 786440 | tf_op jit(solution)/shard_map/ppermute | solution.py:19
  122.5 8.8 %collective-permute-start.14 = (bf16[256,512]{0,1:T(8,128)(2,1)}, bf16[256,512]{0,1:T(8,128)(2,1)}, u32[]{:S(2)}, u32[]{:S(2)}) collective-permute-start(bf16[256,512]{0,1:T(8,128)(2,1)} %collective-permute-done.13), channel_id=1, source_target_pairs={{0,2},{2,4},{4,6},{6,8},{8,10},{10,12},{12,14},{14,16},{16,18},{18... | collective-permute-start | bytes 786440 | tf_op jit(solution)/shard_map/ppermute | solution.py:19
  122.5 14.0 %copy-start.3 = (bf16[256,512]{0,1:T(8,128)(2,1)S(1)}, bf16[256,512]{0,1:T(8,128)(2,1)}, u32[]{:S(2)}) copy-start(bf16[256,512]{0,1:T(8,128)(2,1)} %copy-done.2) | copy-start | bytes 786436
  136.9 8.5 %copy-start.4 = (bf16[256,512]{1,0:T(8,128)(2,1)S(1)}, bf16[256,512]{1,0:T(8,128)(2,1)}, u32[]{:S(2)}) copy-start(bf16[256,512]{1,0:T(8,128)(2,1)} %param.9) | copy-start | bytes 786436
  139.2 52.3 %all-to-all-start = ((bf16[256,2,4096]{0,2,1:T(8,128)(2,1)}), bf16[256,2,4096]{0,2,1:T(8,128)(2,1)}, u32[]{:S(2)}, u32[]{:S(2)}) async-start(bf16[256,2,4096]{0,2,1:T(8,128)(2,1)} %bitcast.28), calls=%async_computation | async-start | bytes 8388608 | tf_op jit(solution)/shard_map/all_to_all | solution.py:48
  144.9 83.7 %collective-permute-start.17 = (bf16[4,512,1024]{2,1,0:T(8,128)(2,1)}, bf16[4,512,1024]{2,1,0:T(8,128)(2,1)}, u32[]{:S(2)}, u32[]{:S(2)}) collective-permute-start(bf16[4,512,1024]{2,1,0:T(8,128)(2,1)} %param.13), channel_id=1, source_target_pairs={{0,2},{2,0},{4,6},{6,4},{8,10},{10,8},{12,14},{14,12},{16,18},{18,... | collective-permute-start | bytes 12582920 | tf_op jit(solution)/shard_map/ppermute | solution.py:26
  145.0 88.2 %collective-permute-start.16 = (bf16[4,512,1024]{2,1,0:T(8,128)(2,1)}, bf16[4,512,1024]{2,1,0:T(8,128)(2,1)}, u32[]{:S(2)}, u32[]{:S(2)}) collective-permute-start(bf16[4,512,1024]{2,1,0:T(8,128)(2,1)} %param.12), channel_id=1, source_target_pairs={{0,2},{2,0},{4,6},{6,4},{8,10},{10,8},{12,14},{14,12},{16,18},{18,... | collective-permute-start | bytes 12582920 | tf_op jit(solution)/shard_map/ppermute | solution.py:26
  204.5 42.4 %collective-permute-start.15 = (bf16[4,1024,512]{2,1,0:T(8,128)(2,1)}, bf16[4,1024,512]{2,1,0:T(8,128)(2,1)}, u32[]{:S(2)}, u32[]{:S(2)}) collective-permute-start(bf16[4,1024,512]{2,1,0:T(8,128)(2,1)} %bitcast.3), channel_id=1, source_target_pairs={{0,2},{2,0},{4,6},{6,4},{8,10},{10,8},{12,14},{14,12},{16,18},{18,... | collective-permute-start | bytes 12582920 | tf_op jit(solution)/shard_map/ppermute | solution.py:26
  204.5 4.5 %copy-start.1 = (bf16[4,512,1024]{2,1,0:T(8,128)(2,1)S(1)}, bf16[4,512,1024]{2,1,0:T(8,128)(2,1)}, u32[]{:S(2)}) copy-start(bf16[4,512,1024]{2,1,0:T(8,128)(2,1)} %param.13) | copy-start | bytes 12582916
  208.9 6.9 %copy-start = (bf16[4,512,1024]{2,1,0:T(8,128)(2,1)S(1)}, bf16[4,512,1024]{2,1,0:T(8,128)(2,1)}, u32[]{:S(2)}) copy-start(bf16[4,512,1024]{2,1,0:T(8,128)(2,1)} %param.12) | copy-start | bytes 12582916
  211.5 6.9 %slice-start = ((s8[8388608]{0:T(1024)(128)(4,1)}), s8[4194304]{0:T(1024)(128)(4,1)S(1)}, s32[]{:S(2)}) async-start(s8[8388608]{0:T(1024)(128)(4,1)} %bitcast.29), calls=%async_computation.1 | async-start | bytes 8388608
  215.9 3.7 %slice-start.1 = ((s8[8388608]{0:T(1024)(128)(4,1)}), s8[4194304]{0:T(1024)(128)(4,1)S(1)}, s32[]{:S(2)}) async-start(s8[8388608]{0:T(1024)(128)(4,1)} %bitcast.29), calls=%async_computation.2 | async-start | bytes 8388608
  215.9 8.2 %slice-start.2 = ((s8[8388608]{0:T(1024)(128)(4,1)}), s8[4194304]{0:T(1024)(128)(4,1)S(1)}, s32[]{:S(2)}) async-start(s8[8388608]{0:T(1024)(128)(4,1)} %bitcast.31), calls=%async_computation.3 | async-start | bytes 8388608
  219.6 4.5 %slice-start.3 = ((s8[8388608]{0:T(1024)(128)(4,1)}), s8[4194304]{0:T(1024)(128)(4,1)S(1)}, s32[]{:S(2)}) async-start(s8[8388608]{0:T(1024)(128)(4,1)} %bitcast.31), calls=%async_computation.4 | async-start | bytes 8388608
  285.6 31.2 %collective-permute-start.18 = (bf16[4,1024,512]{2,1,0:T(8,128)(2,1)}, bf16[4,1024,512]{2,1,0:T(8,128)(2,1)}, u32[]{:S(2)}, u32[]{:S(2)}) collective-permute-start(bf16[4,1024,512]{2,1,0:T(8,128)(2,1)} %get-tuple-element.6), channel_id=1, source_target_pairs={{0,2},{2,0},{4,6},{6,4},{8,10},{10,8},{12,14},{14,12},{16,18},{18,... | collective-permute-start | bytes 12582920 | tf_op jit(solution)/shard_map/ppermute | solution.py:26
